TPU v7x, 128 devices: a whole 4x4x4 slice. The times are simulated.
128 devices in a mesh: grp: 4 (over y), dev: 32 (over z, x, core).
Axes of the slice: x: 4, y: 4, z: 4, core: 2. Of those that a mesh axis runs over, the one named last changes fastest.
Arguments:
- integral_slabs: bfloat16 [32, 512, 512], P('dev'), may hold values from -6 to 6
- slab_owner: int32 [32], replicated, may hold values from 0 to 31, each once
- pair_orbs: int32 [1024, 2], P(('grp', 'dev')), may hold values from 0 to 31, all different within a row; in each aligned block of 8 rows (0 to 7, 8 to 15, ...) at most 2 rows name the same one
- domain_bases: bfloat16 [1024, 512, 128], P(('grp', 'dev')), may hold values from -0.25 to 0.25
- amplitudes: bfloat16 [1024, 128, 128], P(('grp', 'dev')), may hold values from -6 to 6
- coupled: int32 [1024, 32], P(('grp', 'dev')), may hold values from 0 to 31
- coupled_len: int32 [1024], P(('grp', 'dev')), may hold values from 1 to 32, as said below
Outputs:
- residual: float32 [1024, 128, 128], P(('grp', 'dev'))
Inputs may be any that keep to these rules, and one draw needn't show every extreme that they name: `slab_owner`: a permutation of the positions. `pair_orbs`: the two orbitals of a pair differ; among the pairs of one device no orbital is named more than 2 times. `coupled_len`: pair 0 uses all 32 slots.
All inputs are finite; a program needn't handle non-finite values.
Results may differ from a plain program's by a relative error of at most 0.005.
Values may be sent and summed in bfloat16 or wider, within the bound.
A program may use at most 128 MiB of HBM per device.

v0:
```python
import math
import jax
import jax.numpy as jnp
from jax import lax
from jax.sharding import PartitionSpec as P

NAUX = 512
NORB = 512
NPNO = 128


def side_positions(orbitals, slab_owner):
    flat = orbitals.reshape(-1)
    table = jnp.arange(slab_owner.shape[0], dtype=jnp.int32)
    return jnp.sum(jnp.where(flat[:, None] == table[None, :], slab_owner[None, :], 0), axis=1)


def make_fold(positions, slab_piece):
    rows = jnp.arange(slab_piece.shape[0], dtype=jnp.int32)
    select = (positions[:, None] == rows[None, :]).astype(jnp.bfloat16)
    picked = jnp.einsum("sk,kxn->sxn", select, slab_piece, preferred_element_type=jnp.float32)
    return picked.astype(jnp.bfloat16)


def half_pairs(halves):
    pair_count = halves.shape[0] // 2
    paired = halves.reshape(pair_count, 2, halves.shape[1], halves.shape[2])
    inverse_root = 1.0 / math.sqrt(NAUX)
    return (
        jnp.einsum("pan,pam->pnm", paired[:, 0], paired[:, 1], preferred_element_type=jnp.float32)
        * inverse_root
    )


def coupled_part(domain_bases, coupled, coupled_len, cand_bases, cand_amps):
    cand_count = cand_bases.shape[0]
    slot_live = (jnp.arange(coupled.shape[1])[None, :] < coupled_len[:, None]).astype(jnp.float32)
    matches = (
        coupled[:, :, None] == jnp.arange(cand_count, dtype=jnp.int32)[None, None, :]
    ).astype(jnp.float32)
    counts = jnp.einsum("ps,psc->pc", slot_live, matches)

    def one_pair(inputs):
        domain_basis, weights = inputs
        intersection = jnp.einsum(
            "ra,crb->cab", domain_basis, cand_bases, preferred_element_type=jnp.float32
        ).astype(jnp.bfloat16)
        projected = jnp.einsum(
            "cab,cbd->cad", intersection, cand_amps, preferred_element_type=jnp.float32
        ).astype(jnp.bfloat16)
        coupled_terms = jnp.einsum(
            "cad,ced->cae", projected, intersection, preferred_element_type=jnp.float32
        )
        return jnp.einsum("c,cae->ae", weights, coupled_terms)

    return lax.map(one_pair, (domain_bases, counts))


def on_device(
    integral_slabs, slab_owner, pair_orbs, domain_bases, amplitudes, coupled, coupled_len
):
    naux_full = integral_slabs.shape[1]
    norb_full = integral_slabs.shape[2]
    npno = domain_bases.shape[2]
    pair_count = domain_bases.shape[0]
    cand_bases, cand_amps = (
        lax.all_gather(domain_bases, "grp", axis=0, tiled=True),
        lax.all_gather(amplitudes, "grp", axis=0, tiled=True),
    )
    positions = side_positions(pair_orbs, slab_owner)
    side_slabs = make_fold(positions, lax.all_gather(integral_slabs, "dev", axis=0, tiled=True))
    paired_slabs = side_slabs.reshape(pair_count, 2, naux_full, norb_full)
    halves = jnp.einsum(
        "pkxn,pnq->pkxq", paired_slabs, domain_bases, preferred_element_type=jnp.float32
    ).astype(jnp.bfloat16)
    halves = halves.reshape(2 * pair_count, naux_full, npno)
    exchange = half_pairs(halves)
    coupled_sum = coupled_part(domain_bases, coupled, coupled_len, cand_bases, cand_amps)
    return exchange + NORB / NPNO * coupled_sum


def solution(mesh):
    in_specs = (
        P("dev", None, None),
        P(),
        P(("grp", "dev"), None),
        P(("grp", "dev"), None, None),
        P(("grp", "dev"), None, None),
        P(("grp", "dev"), None),
        P(("grp", "dev")),
    )
    out_specs = P(("grp", "dev"), None, None)
    return jax.shard_map(
        on_device, mesh=mesh, in_specs=in_specs, out_specs=out_specs, check_vma=False
    )
```

profile of v0, /device:TPU:1, one launch (start us, length us, event | category | flops | bytes accessed | tf_op | source)
XLA Modules:
  0.0 207.8 jit_solution(17346117150356649458)
XLA Ops:
  6.5 0.7 all-gather.8.cloned.1.call-update
  7.3 0.7 all-gather.6.cloned.1.call-update
  8.1 0.7 all-gather.4.cloned.1.call-update
  8.7 0.8 copy.23
  9.6 0.7 fusion.22
  10.3 0.9 fusion.16
  11.2 0.8 select_reduce_fusion
  12.1 22.2 %all-gather.8.cloned.1.call-done = bf16[32,128,128]{2,1,0:T(8,128)(2,1)} async-done(((bf16[8,128,128]{2,1,0:T(8,128)(2,1)}), bf16[32,128,128]{2,1,0:T(8,128)(2,1)}) %all-gather.8.cloned.1.call-update) | async-done | bytes 1048592 | tf_op jit(solution)/shard_map/all_gather | solution.py:68
  34.3 52.2 %all-gather.6.cloned.1.call-done = bf16[32,512,128]{2,1,0:T(8,128)(2,1)} async-done(((bf16[8,512,128]{2,1,0:T(8,128)(2,1)}), bf16[32,512,128]{2,1,0:T(8,128)(2,1)}) %all-gather.6.cloned.1.call-update) | async-done | bytes 4194320 | tf_op jit(solution)/shard_map/all_gather | solution.py:67
  86.4 49.6 %while.10 = (s32[]{:T(128)}, f32[8,128,128]{2,1,0:T(8,128)S(1)}, bf16[8,32]{1,0:T(8,128)(2,1)S(1)}, bf16[8,512,128]{2,1,0:T(8,128)(2,1)}, bf16[32,512,128]{2,1,0...) while((s32[]{:T(128)}, f32[8,128,128]{2,1,0:T(8,128)S(1)}, bf16[8,32]{1,0:T(8,128)(2,1)S(1)}, ...), condition=%wide.region_2.3_spmd, body=%wide.region_1.2_spmd.sunk | while | flops 807403520 | bytes 9765973 | solution.py:56
  86.4 3.0 %fusion.45 = bf16[32,128,128]{2,1,0:T(8,128)(2,1)S(1)} fusion(bf16[32,512,128]{2,1,0:T(8,128)(2,1)} %get-tuple-element.129, bf16[8,512,128]{2,1,0:T(8,128)(2,1)} %get-tuple-element.128, s32[]{:T(128)} %get-tuple-element.118), kind=kOutput, calls=%fused_computation.4.clone.1 | convolution fusion | flops 537395200 | bytes 5374464 | tf_op jit(solution)/shard_map/while/body/eval_jaxpr/ra,crb->cab/dot_general | solution.py:45
  89.4 2.4 %fusion.46 = bf16[32,128,128]{2,1,0:T(8,128)(2,1)S(1)} fusion(bf16[32,128,128]{2,1,0:T(8,128)(2,1)S(1)} %fusion.45, bf16[32,128,128]{2,1,0:T(8,128)(2,1)} %get-tuple-element.130), kind=kOutput, calls=%fused_computation.5.clone.1 | convolution fusion | flops 268959744 | bytes 3145728 | tf_op jit(solution)/shard_map/while/body/eval_jaxpr/cad,ced->cae/dot_general | solution.py:51
  92.5 3.0 %fusion.45 = bf16[32,128,128]{2,1,0:T(8,128)(2,1)S(1)} fusion(bf16[32,512,128]{2,1,0:T(8,128)(2,1)} %get-tuple-element.129, bf16[8,512,128]{2,1,0:T(8,128)(2,1)} %get-tuple-element.128, s32[]{:T(128)} %get-tuple-element.118), kind=kOutput, calls=%fused_computation.4.clone.1 | convolution fusion | flops 537395200 | bytes 5374464 | tf_op jit(solution)/shard_map/while/body/eval_jaxpr/ra,crb->cab/dot_general | solution.py:45
  95.5 2.4 %fusion.46 = bf16[32,128,128]{2,1,0:T(8,128)(2,1)S(1)} fusion(bf16[32,128,128]{2,1,0:T(8,128)(2,1)S(1)} %fusion.45, bf16[32,128,128]{2,1,0:T(8,128)(2,1)} %get-tuple-element.130), kind=kOutput, calls=%fused_computation.5.clone.1 | convolution fusion | flops 268959744 | bytes 3145728 | tf_op jit(solution)/shard_map/while/body/eval_jaxpr/cad,ced->cae/dot_general | solution.py:51
  98.6 3.3 %fusion.45 = bf16[32,128,128]{2,1,0:T(8,128)(2,1)S(1)} fusion(bf16[32,512,128]{2,1,0:T(8,128)(2,1)} %get-tuple-element.129, bf16[8,512,128]{2,1,0:T(8,128)(2,1)} %get-tuple-element.128, s32[]{:T(128)} %get-tuple-element.118), kind=kOutput, calls=%fused_computation.4.clone.1 | convolution fusion | flops 537395200 | bytes 5374464 | tf_op jit(solution)/shard_map/while/body/eval_jaxpr/ra,crb->cab/dot_general | solution.py:45
  101.9 2.4 %fusion.46 = bf16[32,128,128]{2,1,0:T(8,128)(2,1)S(1)} fusion(bf16[32,128,128]{2,1,0:T(8,128)(2,1)S(1)} %fusion.45, bf16[32,128,128]{2,1,0:T(8,128)(2,1)} %get-tuple-element.130), kind=kOutput, calls=%fused_computation.5.clone.1 | convolution fusion | flops 268959744 | bytes 3145728 | tf_op jit(solution)/shard_map/while/body/eval_jaxpr/cad,ced->cae/dot_general | solution.py:51
  104.3 0.7 fusion.47
  105.0 3.1 %fusion.45 = bf16[32,128,128]{2,1,0:T(8,128)(2,1)S(1)} fusion(bf16[32,512,128]{2,1,0:T(8,128)(2,1)} %get-tuple-element.129, bf16[8,512,128]{2,1,0:T(8,128)(2,1)} %get-tuple-element.128, s32[]{:T(128)} %get-tuple-element.118), kind=kOutput, calls=%fused_computation.4.clone.1 | convolution fusion | flops 537395200 | bytes 5374464 | tf_op jit(solution)/shard_map/while/body/eval_jaxpr/ra,crb->cab/dot_general | solution.py:45
  108.1 2.4 %fusion.46 = bf16[32,128,128]{2,1,0:T(8,128)(2,1)S(1)} fusion(bf16[32,128,128]{2,1,0:T(8,128)(2,1)S(1)} %fusion.45, bf16[32,128,128]{2,1,0:T(8,128)(2,1)} %get-tuple-element.130), kind=kOutput, calls=%fused_computation.5.clone.1 | convolution fusion | flops 268959744 | bytes 3145728 | tf_op jit(solution)/shard_map/while/body/eval_jaxpr/cad,ced->cae/dot_general | solution.py:51
  111.2 3.0 %fusion.45 = bf16[32,128,128]{2,1,0:T(8,128)(2,1)S(1)} fusion(bf16[32,512,128]{2,1,0:T(8,128)(2,1)} %get-tuple-element.129, bf16[8,512,128]{2,1,0:T(8,128)(2,1)} %get-tuple-element.128, s32[]{:T(128)} %get-tuple-element.118), kind=kOutput, calls=%fused_computation.4.clone.1 | convolution fusion | flops 537395200 | bytes 5374464 | tf_op jit(solution)/shard_map/while/body/eval_jaxpr/ra,crb->cab/dot_general | solution.py:45
  114.2 2.4 %fusion.46 = bf16[32,128,128]{2,1,0:T(8,128)(2,1)S(1)} fusion(bf16[32,128,128]{2,1,0:T(8,128)(2,1)S(1)} %fusion.45, bf16[32,128,128]{2,1,0:T(8,128)(2,1)} %get-tuple-element.130), kind=kOutput, calls=%fused_computation.5.clone.1 | convolution fusion | flops 268959744 | bytes 3145728 | tf_op jit(solution)/shard_map/while/body/eval_jaxpr/cad,ced->cae/dot_general | solution.py:51
  117.3 3.0 %fusion.45 = bf16[32,128,128]{2,1,0:T(8,128)(2,1)S(1)} fusion(bf16[32,512,128]{2,1,0:T(8,128)(2,1)} %get-tuple-element.129, bf16[8,512,128]{2,1,0:T(8,128)(2,1)} %get-tuple-element.128, s32[]{:T(128)} %get-tuple-element.118), kind=kOutput, calls=%fused_computation.4.clone.1 | convolution fusion | flops 537395200 | bytes 5374464 | tf_op jit(solution)/shard_map/while/body/eval_jaxpr/ra,crb->cab/dot_general | solution.py:45
  120.3 2.4 %fusion.46 = bf16[32,128,128]{2,1,0:T(8,128)(2,1)S(1)} fusion(bf16[32,128,128]{2,1,0:T(8,128)(2,1)S(1)} %fusion.45, bf16[32,128,128]{2,1,0:T(8,128)(2,1)} %get-tuple-element.130), kind=kOutput, calls=%fused_computation.5.clone.1 | convolution fusion | flops 268959744 | bytes 3145728 | tf_op jit(solution)/shard_map/while/body/eval_jaxpr/cad,ced->cae/dot_general | solution.py:51
  123.4 3.1 %fusion.45 = bf16[32,128,128]{2,1,0:T(8,128)(2,1)S(1)} fusion(bf16[32,512,128]{2,1,0:T(8,128)(2,1)} %get-tuple-element.129, bf16[8,512,128]{2,1,0:T(8,128)(2,1)} %get-tuple-element.128, s32[]{:T(128)} %get-tuple-element.118), kind=kOutput, calls=%fused_computation.4.clone.1 | convolution fusion | flops 537395200 | bytes 5374464 | tf_op jit(solution)/shard_map/while/body/eval_jaxpr/ra,crb->cab/dot_general | solution.py:45
  126.5 2.4 %fusion.46 = bf16[32,128,128]{2,1,0:T(8,128)(2,1)S(1)} fusion(bf16[32,128,128]{2,1,0:T(8,128)(2,1)S(1)} %fusion.45, bf16[32,128,128]{2,1,0:T(8,128)(2,1)} %get-tuple-element.130), kind=kOutput, calls=%fused_computation.5.clone.1 | convolution fusion | flops 268959744 | bytes 3145728 | tf_op jit(solution)/shard_map/while/body/eval_jaxpr/cad,ced->cae/dot_general | solution.py:51
  129.6 3.1 %fusion.45 = bf16[32,128,128]{2,1,0:T(8,128)(2,1)S(1)} fusion(bf16[32,512,128]{2,1,0:T(8,128)(2,1)} %get-tuple-element.129, bf16[8,512,128]{2,1,0:T(8,128)(2,1)} %get-tuple-element.128, s32[]{:T(128)} %get-tuple-element.118), kind=kOutput, calls=%fused_computation.4.clone.1 | convolution fusion | flops 537395200 | bytes 5374464 | tf_op jit(solution)/shard_map/while/body/eval_jaxpr/ra,crb->cab/dot_general | solution.py:45
  132.7 2.4 %fusion.46 = bf16[32,128,128]{2,1,0:T(8,128)(2,1)S(1)} fusion(bf16[32,128,128]{2,1,0:T(8,128)(2,1)S(1)} %fusion.45, bf16[32,128,128]{2,1,0:T(8,128)(2,1)} %get-tuple-element.130), kind=kOutput, calls=%fused_computation.5.clone.1 | convolution fusion | flops 268959744 | bytes 3145728 | tf_op jit(solution)/shard_map/while/body/eval_jaxpr/cad,ced->cae/dot_general | solution.py:51
  136.0 26.3 %all-gather.4.cloned.1.call-done = bf16[32,512,512]{2,1,0:T(8,128)(2,1)} async-done(((bf16[1,512,512]{2,1,0:T(8,128)(2,1)}), bf16[32,512,512]{2,1,0:T(8,128)(2,1)}) %all-gather.4.cloned.1.call-update) | async-done | bytes 16777232 | tf_op jit(solution)/shard_map/all_gather | solution.py:71
  162.3 20.3 %fusion.11 = bf16[16,512,512]{2,0,1:T(8,128)(2,1)} fusion(bf16[32,512,512]{2,1,0:T(8,128)(2,1)} %all-gather.4.cloned.1.call-done, s32[16]{0:T(128)S(1)} %select_reduce_fusion), kind=kOutput, calls=%fused_computation.14 | convolution fusion | flops 272630272 | bytes 25165888 | tf_op jit(solution)/shard_map/sk,kxn->sxn/dot_general | solution.py:21
  182.6 11.7 %copy.34 = bf16[16,512,512]{2,1,0:T(8,128)(2,1)} copy(bf16[16,512,512]{2,0,1:T(8,128)(2,1)} %fusion.11) | data formatting | bytes 16777216 | tf_op jit(solution)/shard_map/reshape | solution.py:72
  194.2 5.7 %convolution_convert_fusion.2 = bf16[8,2,512,128]{3,2,1,0:T(8,128)(2,1)S(1)} fusion(bf16[8,2,512,512]{3,2,1,0:T(8,128)(2,1)} %bitcast.55, bf16[8,512,128]{2,1,0:T(8,128)(2,1)S(1)} %copy-done), kind=kOutput, calls=%fused_computation.15 | convolution fusion | flops 1074790400 | bytes 11534336 | tf_op jit(solution)/shard_map/pkxn,pnq->pkxq/dot_general | solution.py:73
  200.0 1.3 fusion.14
  (23 shorter events, 5.0 us)
Async XLA Ops:
  6.5 27.7 %all-gather.8.cloned.1.call-start = ((), (), s32[]{:S(2)}) async-start(), calls=%async_computation.2 | async-start | bytes 1310720 | tf_op jit(solution)/shard_map/all_gather | solution.py:68
  7.3 79.2 %all-gather.6.cloned.1.call-start = ((), (), s32[]{:S(2)}) async-start(), calls=%async_computation.1 | async-start | bytes 5242880 | tf_op jit(solution)/shard_map/all_gather | solution.py:67
  8.0 154.3 %all-gather.4.cloned.1.call-start = ((), (), s32[]{:S(2)}) async-start(), calls=%async_computation | async-start | bytes 17301504 | tf_op jit(solution)/shard_map/all_gather | solution.py:71
  182.6 11.7 %copy-start = (bf16[8,512,128]{2,1,0:T(8,128)(2,1)S(1)}, bf16[8,512,128]{2,1,0:T(8,128)(2,1)}, u32[]{:S(2)}) copy-start(bf16[8,512,128]{2,1,0:T(8,128)(2,1)} %get-tuple-element.140) | copy-start | bytes 3145732
Sparse Core Ops, SparseCore 0:
  9.0 25.2 all-gather.7
  35.9 50.4 all-gather.5
  88.7 73.5 all-gather.3
where the time goes:
time: 208 us
  waiting for transfers between devices  103 us (50%)
  matrix products  77.3 us (37%)
  between operations  13.1 us (6%)
  local copies, waits for them, and re-layouts  12.6 us (6%)
    all_gather x1, waiting for transfers between devices, on_device(): lax.all_gather(domain_bases, 'grp', axis=0, tiled=True)  52.2 us
    all_gather x1, waiting for transfers between devices, on_device(): lax.all_gather(integral_slabs, 'dev', axis=0, tiled=True)  26.3 us
    dot_general x8, matrix products, one_pair(): jnp.einsum('ra,crb->cab', domain_basis, cand_bases, preferred_element_typ...  24.7 us
    all_gather x1, waiting for transfers between devices, on_device(): lax.all_gather(amplitudes, 'grp', axis=0, tiled=True)  22.2 us
    dot_general x1, matrix products, make_fold(): jnp.einsum('sk,kxn->sxn', select, slab_piece, preferred_element_type=jnp....  20.3 us
    dot_general x8, matrix products, one_pair(): jnp.einsum('cad,ced->cae', projected, intersection, preferred_element_typ...  19.1 us
    reshape x1, local copies, waits for them, and re-layouts, on_device(): paired_slabs = side_slabs.reshape(pair_count, 2, naux_full, norb_full)  11.7 us
    dot_general x1, matrix products, on_device(): jnp.einsum('pkxn,pnq->pkxq', paired_slabs, domain_bases, preferred_elemen...  5.71 us
  transfers between devices with their start and end apart: 3, of which 3 were waited for; matrix products, arithmetic and copies ran while one was open for 25% of the time, Pallas kernels for 0%

commit v1 on v0

--- a/solution.py
+++ b/solution.py
@@ -7,6 +7,13 @@
 NAUX = 512
 NORB = 512
 NPNO = 128
+
+
+def swapped_in(x, axis, along):
+    size = lax.axis_size(axis)
+    blocks = jnp.stack([x for _ in range(size)])
+    blocks = lax.all_to_all(blocks, axis, split_axis=0, concat_axis=0)
+    return jnp.concatenate(blocks, axis=along)
 
 
 def side_positions(orbitals, slab_owner):
@@ -65,7 +72,7 @@
     pair_count = domain_bases.shape[0]
     cand_bases, cand_amps = (
         lax.all_gather(domain_bases, "grp", axis=0, tiled=True),
-        lax.all_gather(amplitudes, "grp", axis=0, tiled=True),
+        swapped_in(amplitudes, "grp", 0),
     )
     positions = side_positions(pair_orbs, slab_owner)
     side_slabs = make_fold(positions, lax.all_gather(integral_slabs, "dev", axis=0, tiled=True))

time: 208 us -> 187 us (0.90)
  waiting for transfers between devices: 103 us -> 79 us
  matrix products: 77.3 us -> 67.3 us
  local copies, waits for them, and re-layouts: 12.6 us -> 19.8 us
  starting transfers between devices: 0.08 us -> 5.04 us
    all_gather x1 -> x0, waiting for transfers between devices: 22.2 us -> none  [on_device(): lax.all_gather(amplitudes, 'grp', axis=0, tiled=True)]
    all_gather x1, waiting for transfers between devices: 52.2 us -> 32.9 us  [on_device(): lax.all_gather(domain_bases, 'grp', axis=0, tiled=True)]
    all_to_all x0 -> x1, waiting for transfers between devices: none -> 13.4 us  [swapped_in(): blocks = lax.all_to_all(blocks, axis, split_axis=0, concat_axis=0)]
    dot_general x8, matrix products: 19.1 us -> 9.2 us  [one_pair(): jnp.einsum('cad,ced->cae', projected, intersection, preferred_element_typ...]
    all_gather x1, waiting for transfers between devices: 26.3 us -> 31.3 us  [on_device(): lax.all_gather(integral_slabs, 'dev', axis=0, tiled=True)]
    dynamic_update_slice x8, local copies, waits for them, and re-layouts: 0.07 us -> 5.1 us  [coupled_part(): return lax.map(one_pair, (domain_bases, counts))]
    all_to_all x0 -> x1, starting transfers between devices: none -> 5 us  [swapped_in(): blocks = lax.all_to_all(blocks, axis, split_axis=0, concat_axis=0)]
    another operation x0 -> x1, local copies, waits for them, and re-layouts: none -> 2.16 us  [swapped_in(): blocks = jnp.stack([x for _ in range(size)])]
  transfers between devices with their start and end apart: 3 -> 3, of which waited for: 3 -> 3; matrix products, arithmetic and copies ran while one was open for 25% -> 27% of each run, Pallas kernels for 0% -> 0%
where the time goes in v1:
time: 187 us; the launch traced here: 186 us
  waiting for transfers between devices  79 us (42%)
  matrix products  67.3 us (36%)
  local copies, waits for them, and re-layouts  19.8 us (11%)
  between operations  13.4 us (7%)
  starting transfers between devices  5.04 us (3%)
    all_gather x1, waiting for transfers between devices, on_device(): lax.all_gather(domain_bases, 'grp', axis=0, tiled=True)  32.9 us
    all_gather x1, waiting for transfers between devices, on_device(): lax.all_gather(integral_slabs, 'dev', axis=0, tiled=True)  31.3 us
    dot_general x8, matrix products, one_pair(): jnp.einsum('ra,crb->cab', domain_basis, cand_bases, preferred_element_typ...  24.5 us
    dot_general x1, matrix products, make_fold(): jnp.einsum('sk,kxn->sxn', select, slab_piece, preferred_element_type=jnp....  20.3 us
    all_to_all x1, waiting for transfers between devices, swapped_in(): blocks = lax.all_to_all(blocks, axis, split_axis=0, concat_axis=0)  13.4 us
    reshape x1, local copies, waits for them, and re-layouts, on_device(): paired_slabs = side_slabs.reshape(pair_count, 2, naux_full, norb_full)  11.7 us
    dot_general x8, matrix products, one_pair(): jnp.einsum('cad,ced->cae', projected, intersection, preferred_element_typ...  9.2 us
    dot_general x1, matrix products, on_device(): jnp.einsum('pkxn,pnq->pkxq', paired_slabs, domain_bases, preferred_elemen...  5.77 us
  transfers between devices with their start and end apart: 3, of which 3 were waited for; matrix products, arithmetic and copies ran while one was open for 27% of the time, Pallas kernels for 0%

profile of v1, /device:TPU:1, one launch (start us, length us, event | category | flops | bytes accessed | tf_op | source)
XLA Modules:
  0.0 186.2 jit_solution(15276243137111669447)
XLA Ops:
  6.5 0.7 all-gather.5.cloned.1.call-update
  7.3 0.7 all-gather.3.cloned.1.call-update
  8.0 2.2 %stack.2 = bf16[4,8,128,128]{3,2,1,0:T(8,128)(2,1)} broadcast(bf16[8,128,128]{2,1,0:T(8,128)(2,1)} %param.13), dimensions={1,2,3} | broadcast | bytes 1310720 | tf_op jit(solution)/shard_map/stack | solution.py:14
  10.2 5.0 %all-to-all-start = ((bf16[4,8,128,128]{3,2,1,0:T(8,128)(2,1)}), bf16[4,8,128,128]{3,2,1,0:T(8,128)(2,1)S(1)}, u32[]{:S(2)}, u32[]{:S(2)}) async-start(bf16[4,8,128,128]{3,2,1,0:T(8,128)(2,1)} %stack.2), calls=%async_computation | async-start | bytes 2097152 | tf_op jit(solution)/shard_map/all_to_all | solution.py:15
  15.2 0.8 copy.23
  16.0 0.7 fusion.22
  16.7 0.9 fusion.16
  17.6 0.8 select_reduce_fusion
  18.5 13.4 %all-to-all-done = bf16[4,8,128,128]{3,2,1,0:T(8,128)(2,1)S(1)} async-done(((bf16[4,8,128,128]{3,2,1,0:T(8,128)(2,1)}), bf16[4,8,128,128]{3,2,1,0:T(8,128)(2,1)S(1)}, u32[]{:S(2)}, u32[]{:S(2)}) %all-to-all-start) | async-done | bytes 1048608 | tf_op jit(solution)/shard_map/all_to_all | solution.py:15
  31.8 32.9 %all-gather.5.cloned.1.call-done = bf16[32,512,128]{2,1,0:T(8,128)(2,1)} async-done(((bf16[8,512,128]{2,1,0:T(8,128)(2,1)}), bf16[32,512,128]{2,1,0:T(8,128)(2,1)}) %all-gather.5.cloned.1.call-update) | async-done | bytes 4194320 | tf_op jit(solution)/shard_map/all_gather | solution.py:74
  64.8 44.2 %while.10 = (s32[]{:T(128)}, f32[8,128,128]{2,1,0:T(8,128)}, bf16[8,32]{1,0:T(8,128)(2,1)S(1)}, bf16[8,512,128]{2,1,0:T(8,128)(2,1)}, bf16[32,512,128]{2,1,0:T(8...) while((s32[]{:T(128)}, f32[8,128,128]{2,1,0:T(8,128)}, bf16[8,32]{1,0:T(8,128)(2,1)S(1)}, ...), condition=%wide.region_2.3_spmd, body=%wide.region_1.2_spmd.sunk | while | flops 807403520 | bytes 9766481 | solution.py:63
  64.8 3.0 %fusion.45 = bf16[32,128,128]{2,1,0:T(8,128)(2,1)S(1)} fusion(bf16[32,512,128]{2,1,0:T(8,128)(2,1)} %get-tuple-element.129, bf16[8,512,128]{2,1,0:T(8,128)(2,1)} %get-tuple-element.128, s32[]{:T(128)} %get-tuple-element.118), kind=kOutput, calls=%fused_computation.4.clone.1 | convolution fusion | flops 537395200 | bytes 5374464 | tf_op jit(solution)/shard_map/while/body/eval_jaxpr/ra,crb->cab/dot_general | solution.py:52
  67.8 1.2 fusion.46
  70.3 3.0 %fusion.45 = bf16[32,128,128]{2,1,0:T(8,128)(2,1)S(1)} fusion(bf16[32,512,128]{2,1,0:T(8,128)(2,1)} %get-tuple-element.129, bf16[8,512,128]{2,1,0:T(8,128)(2,1)} %get-tuple-element.128, s32[]{:T(128)} %get-tuple-element.118), kind=kOutput, calls=%fused_computation.4.clone.1 | convolution fusion | flops 537395200 | bytes 5374464 | tf_op jit(solution)/shard_map/while/body/eval_jaxpr/ra,crb->cab/dot_general | solution.py:52
  73.3 1.2 fusion.46
  75.7 3.3 %fusion.45 = bf16[32,128,128]{2,1,0:T(8,128)(2,1)S(1)} fusion(bf16[32,512,128]{2,1,0:T(8,128)(2,1)} %get-tuple-element.129, bf16[8,512,128]{2,1,0:T(8,128)(2,1)} %get-tuple-element.128, s32[]{:T(128)} %get-tuple-element.118), kind=kOutput, calls=%fused_computation.4.clone.1 | convolution fusion | flops 537395200 | bytes 5374464 | tf_op jit(solution)/shard_map/while/body/eval_jaxpr/ra,crb->cab/dot_general | solution.py:52
  79.1 1.2 fusion.46
  81.5 3.0 %fusion.45 = bf16[32,128,128]{2,1,0:T(8,128)(2,1)S(1)} fusion(bf16[32,512,128]{2,1,0:T(8,128)(2,1)} %get-tuple-element.129, bf16[8,512,128]{2,1,0:T(8,128)(2,1)} %get-tuple-element.128, s32[]{:T(128)} %get-tuple-element.118), kind=kOutput, calls=%fused_computation.4.clone.1 | convolution fusion | flops 537395200 | bytes 5374464 | tf_op jit(solution)/shard_map/while/body/eval_jaxpr/ra,crb->cab/dot_general | solution.py:52
  84.6 1.2 fusion.46
  87.0 3.1 %fusion.45 = bf16[32,128,128]{2,1,0:T(8,128)(2,1)S(1)} fusion(bf16[32,512,128]{2,1,0:T(8,128)(2,1)} %get-tuple-element.129, bf16[8,512,128]{2,1,0:T(8,128)(2,1)} %get-tuple-element.128, s32[]{:T(128)} %get-tuple-element.118), kind=kOutput, calls=%fused_computation.4.clone.1 | convolution fusion | flops 537395200 | bytes 5374464 | tf_op jit(solution)/shard_map/while/body/eval_jaxpr/ra,crb->cab/dot_general | solution.py:52
  90.1 1.1 fusion.46
  92.6 3.0 %fusion.45 = bf16[32,128,128]{2,1,0:T(8,128)(2,1)S(1)} fusion(bf16[32,512,128]{2,1,0:T(8,128)(2,1)} %get-tuple-element.129, bf16[8,512,128]{2,1,0:T(8,128)(2,1)} %get-tuple-element.128, s32[]{:T(128)} %get-tuple-element.118), kind=kOutput, calls=%fused_computation.4.clone.1 | convolution fusion | flops 537395200 | bytes 5374464 | tf_op jit(solution)/shard_map/while/body/eval_jaxpr/ra,crb->cab/dot_general | solution.py:52
  95.6 1.2 fusion.46
  98.1 3.0 %fusion.45 = bf16[32,128,128]{2,1,0:T(8,128)(2,1)S(1)} fusion(bf16[32,512,128]{2,1,0:T(8,128)(2,1)} %get-tuple-element.129, bf16[8,512,128]{2,1,0:T(8,128)(2,1)} %get-tuple-element.128, s32[]{:T(128)} %get-tuple-element.118), kind=kOutput, calls=%fused_computation.4.clone.1 | convolution fusion | flops 537395200 | bytes 5374464 | tf_op jit(solution)/shard_map/while/body/eval_jaxpr/ra,crb->cab/dot_general | solution.py:52
  101.1 1.1 fusion.46
  103.5 3.0 %fusion.45 = bf16[32,128,128]{2,1,0:T(8,128)(2,1)S(1)} fusion(bf16[32,512,128]{2,1,0:T(8,128)(2,1)} %get-tuple-element.129, bf16[8,512,128]{2,1,0:T(8,128)(2,1)} %get-tuple-element.128, s32[]{:T(128)} %get-tuple-element.118), kind=kOutput, calls=%fused_computation.4.clone.1 | convolution fusion | flops 537395200 | bytes 5374464 | tf_op jit(solution)/shard_map/while/body/eval_jaxpr/ra,crb->cab/dot_general | solution.py:52
  106.5 1.2 fusion.46
  109.0 31.3 %all-gather.3.cloned.1.call-done = bf16[32,512,512]{2,1,0:T(8,128)(2,1)} async-done(((bf16[1,512,512]{2,1,0:T(8,128)(2,1)}), bf16[32,512,512]{2,1,0:T(8,128)(2,1)}) %all-gather.3.cloned.1.call-update) | async-done | bytes 16777232 | tf_op jit(solution)/shard_map/all_gather | solution.py:78
  140.3 20.3 %fusion.11 = bf16[16,512,512]{2,0,1:T(8,128)(2,1)} fusion(bf16[32,512,512]{2,1,0:T(8,128)(2,1)} %all-gather.3.cloned.1.call-done, s32[16]{0:T(128)S(1)} %select_reduce_fusion), kind=kOutput, calls=%fused_computation.14 | convolution fusion | flops 272630272 | bytes 25165888 | tf_op jit(solution)/shard_map/sk,kxn->sxn/dot_general | solution.py:28
  160.6 11.7 %copy.34 = bf16[16,512,512]{2,1,0:T(8,128)(2,1)} copy(bf16[16,512,512]{2,0,1:T(8,128)(2,1)} %fusion.11) | data formatting | bytes 16777216 | tf_op jit(solution)/shard_map/reshape | solution.py:79
  172.3 5.8 %convolution_convert_fusion.2 = bf16[8,2,512,128]{3,2,1,0:T(8,128)(2,1)S(1)} fusion(bf16[8,2,512,512]{3,2,1,0:T(8,128)(2,1)} %bitcast.57, bf16[8,512,128]{2,1,0:T(8,128)(2,1)S(1)} %copy-done), kind=kOutput, calls=%fused_computation.15 | convolution fusion | flops 1074790400 | bytes 11534336 | tf_op jit(solution)/shard_map/pkxn,pnq->pkxq/dot_general | solution.py:80
  178.1 1.3 fusion.14
  (25 shorter events, 10.6 us)
Async XLA Ops:
  6.5 58.2 %all-gather.5.cloned.1.call-start = ((), (), s32[]{:S(2)}) async-start(), calls=%async_computation.2 | async-start | bytes 5242880 | tf_op jit(solution)/shard_map/all_gather | solution.py:74
  7.3 133.1 %all-gather.3.cloned.1.call-start = ((), (), s32[]{:S(2)}) async-start(), calls=%async_computation.1 | async-start | bytes 17301504 | tf_op jit(solution)/shard_map/all_gather | solution.py:78
  10.2 21.7 %all-to-all-start = ((bf16[4,8,128,128]{3,2,1,0:T(8,128)(2,1)}), bf16[4,8,128,128]{3,2,1,0:T(8,128)(2,1)S(1)}, u32[]{:S(2)}, u32[]{:S(2)}) async-start(bf16[4,8,128,128]{3,2,1,0:T(8,128)(2,1)} %stack.2), calls=%async_computation | async-start | bytes 2097152 | tf_op jit(solution)/shard_map/all_to_all | solution.py:15
  160.6 11.7 %copy-start = (bf16[8,512,128]{2,1,0:T(8,128)(2,1)S(1)}, bf16[8,512,128]{2,1,0:T(8,128)(2,1)}, u32[]{:S(2)}) copy-start(bf16[8,512,128]{2,1,0:T(8,128)(2,1)} %get-tuple-element.139) | copy-start | bytes 3145732
  172.3 5.8 %copy-start.1 = (f32[8,128,128]{2,1,0:T(8,128)S(1)}, f32[8,128,128]{2,1,0:T(8,128)}, u32[]{:S(2)}) copy-start(f32[8,128,128]{2,1,0:T(8,128)} %get-tuple-element.37) | copy-start | bytes 1572868
Sparse Core Ops, SparseCore 0:
  9.0 55.7 all-gather.4
  67.0 73.2 all-gather.2
